TPU v7x, 32 devices: a whole 2x2x4 slice. The times are simulated.
32 devices in a mesh: groups: 2 (over y), row: 4 (over z), col: 2 (over x), sub: 2 (over core).
Axes of the slice: x: 2, y: 2, z: 4, core: 2. Of those that a mesh axis runs over, the one named last changes fastest.
Arguments:
- stream_in: bfloat16 [4096, 5376], P(('groups', 'row'), ('col', 'sub')), parts along dimension 0, may hold values from -6 to 6
- in_gain: float32 [5376], replicated, may hold values from 0.1 to 1.9
- query_weight: bfloat16 [5376, 4096], P('row', ('col', 'sub')), may hold values from -0.078125 to 0.078125
- key_matrix: bfloat16 [5376, 2048], P('row', ('col', 'sub')), may hold values from -0.078125 to 0.078125
- value_matrix: bfloat16 [5376, 2048], P('row', ('col', 'sub')), may hold values from -0.078125 to 0.078125
- query_gain: float32 [128], replicated, may hold values from 0.45 to 10, as said below
- key_norm_gain: float32 [128], replicated, may hold values from 0.45 to 10, as said below
- output_weight: bfloat16 [4096, 5376], P('row', ('col', 'sub')), may hold values from -3 to 3
- post_gain: float32 [5376], P(('col', 'sub')), may hold values from 0.1 to 1.9
Outputs:
- stream_out: bfloat16 [4096, 5376], P(('groups', 'row'), ('col', 'sub')), parts along dimension 0
There are 2 independent parts, one for each index of `groups`. A program takes and returns all parts, laid end to end along the dimension named above; an argument that names none is the same for every part. Nothing has to cross between parts.
Inputs may be any that keep to these rules, and one draw needn't show every extreme that they name: `query_gain`: positive. `key_norm_gain`: positive.
All inputs are finite; a program needn't handle non-finite values.
Results may differ from a plain program's by a relative error of at most 0.014.
The roundings to bfloat16 on the way count: a program that leaves them out, or rounds other values in their place, can miss the bound.
Values may be sent and summed in bfloat16 or wider, within the bound.
A program may use at most 128 MiB of HBM per device.

v0:
```python
import jax
import jax.numpy as jnp
from jax import lax
from jax.sharding import PartitionSpec as P

MODEL_WIDTH = 5376
QUERY_HEAD_COUNT = 32
WINDOW_LENGTH = 1024
EPSILON = 1e-06


def shifted(x, axis, by):
    count = lax.axis_size(axis)
    pairs = [(i, i + by) for i in range(count) if 0 <= i + by < count]
    return lax.ppermute(x, axis, pairs)


def root_mean_scale(values, gain):
    return values * lax.rsqrt(jnp.mean(values * values, axis=-1, keepdims=True) + EPSILON) * gain


def apply_rotary(tensor, token_positions):
    half_dim = tensor.shape[-1] // 2
    inverse = 10000.0 ** (-(jnp.arange(half_dim, dtype=jnp.float32) * 2.0) / tensor.shape[-1])
    angles = token_positions[:, None] * inverse[None, :]
    cosine = jnp.cos(angles)[:, None, :]
    sine_part = jnp.sin(angles)[:, None, :]
    first_half = tensor[..., :half_dim]
    second_half = tensor[..., half_dim:]
    return jnp.concatenate(
        [
            first_half * cosine - second_half * sine_part,
            second_half * cosine + first_half * sine_part,
        ],
        axis=-1,
    )


def on_device(
    stream_in,
    in_gain,
    query_weight,
    key_matrix,
    value_matrix,
    query_gain,
    key_norm_gain,
    output_weight,
    post_gain,
):
    token_rows = lax.all_gather(stream_in, ("col", "sub"), axis=1, tiled=True)
    tokens = token_rows.shape[0]
    normed = root_mean_scale(token_rows.astype(jnp.float32), in_gain).astype(jnp.bfloat16)

    def add_panel(panel_piece):
        return jnp.dot(normed, panel_piece, preferred_element_type=jnp.float32)

    query_proj = add_panel(lax.all_gather(query_weight, "row", axis=0, tiled=True))
    projected_keys = add_panel(lax.all_gather(key_matrix, "row", axis=0, tiled=True))
    projected_values = add_panel(lax.all_gather(value_matrix, "row", axis=0, tiled=True))
    head_size = query_gain.shape[0]
    query_heads = query_weight.shape[1] // head_size
    pair_heads = key_matrix.shape[1] // head_size
    group_count = query_heads // pair_heads
    scale_factor = float(MODEL_WIDTH // QUERY_HEAD_COUNT) ** (-0.5)
    row_index = lax.axis_index("row")
    query_places = row_index * tokens + jnp.arange(tokens, dtype=jnp.int32)
    query_rot = apply_rotary(
        root_mean_scale(query_proj.reshape(tokens, query_heads, head_size), query_gain),
        query_places.astype(jnp.float32),
    ).astype(jnp.bfloat16)
    rotary_keys = apply_rotary(
        root_mean_scale(projected_keys.reshape(tokens, pair_heads, head_size), key_norm_gain),
        query_places.astype(jnp.float32),
    ).astype(jnp.bfloat16)
    keys_flat = rotary_keys.reshape(tokens, pair_heads * head_size)
    values_flat = projected_values.astype(jnp.bfloat16)
    shards_back = min(WINDOW_LENGTH // tokens, lax.axis_size("row") - 1)
    band_length = (shards_back + 1) * tokens
    key_parts = [keys_flat]
    value_parts = [values_flat]
    for offset in range(1, shards_back + 1):
        keys_prior, values_prior = shifted((keys_flat, values_flat), "row", offset)
        key_parts = [keys_prior] + key_parts
        value_parts = [values_prior] + value_parts
    keys_band = jnp.concatenate(key_parts, axis=0)
    values_band = jnp.concatenate(value_parts, axis=0)
    key_places = (row_index - shards_back) * tokens + jnp.arange(band_length, dtype=jnp.int32)
    distance = query_places[:, None] - key_places[None, :]
    visible = (distance >= 0) & (distance < WINDOW_LENGTH) & (key_places[None, :] >= 0)
    grouped = query_rot.reshape(tokens, pair_heads, group_count, head_size)
    scores = (
        jnp.einsum(
            "qhgd,shd->hgqs",
            grouped,
            keys_band.reshape(band_length, pair_heads, head_size),
            preferred_element_type=jnp.float32,
        )
        * scale_factor
    )
    scores = jnp.where(visible, scores, -1e30)
    row_max = jnp.max(scores, axis=-1, keepdims=True)
    exponent = jnp.exp(scores - row_max)
    weights = (exponent / jnp.sum(exponent, axis=-1, keepdims=True)).astype(jnp.bfloat16)
    attended = jnp.einsum(
        "hgqs,shd->qhgd",
        weights,
        values_band.reshape(band_length, pair_heads, head_size),
        preferred_element_type=jnp.float32,
    )
    heads_out = attended.reshape(tokens, query_heads * head_size).astype(jnp.bfloat16)
    head_rows = lax.all_gather(heads_out, ("col", "sub"), axis=1, tiled=True)
    branch = jnp.dot(
        head_rows,
        lax.all_gather(output_weight, "row", axis=0, tiled=True),
        preferred_element_type=jnp.float32,
    )
    squares = lax.psum(jnp.sum(branch * branch, axis=-1), ("col", "sub"))
    scaled = branch * lax.rsqrt(squares[:, None] / MODEL_WIDTH + EPSILON) * post_gain
    return (stream_in.astype(jnp.float32) + scaled).astype(jnp.bfloat16)


def swapped(x):
    count = lax.axis_size("groups")
    return lax.ppermute(x, "groups", [(i, count - 1 - i) for i in range(count)])


def rows_gathered(piece):
    return lax.all_gather(piece, "row", axis=0)


def attend(query_rot, keys_flat, values_flat, row_index, head_size, scale_factor):
    tokens, kv_width = keys_flat.shape
    pair_heads = kv_width // head_size
    group_count = query_rot.shape[1] // pair_heads
    query_places = row_index * tokens + jnp.arange(tokens, dtype=jnp.int32)
    shards_back = min(WINDOW_LENGTH // tokens, lax.axis_size("row") - 1)
    band_length = (shards_back + 1) * tokens
    key_parts = [keys_flat]
    value_parts = [values_flat]
    for offset in range(1, shards_back + 1):
        keys_prior, values_prior = shifted((keys_flat, values_flat), "row", offset)
        key_parts = [keys_prior] + key_parts
        value_parts = [values_prior] + value_parts
    keys_band = jnp.concatenate(key_parts, axis=0)
    values_band = jnp.concatenate(value_parts, axis=0)
    key_places = (row_index - shards_back) * tokens + jnp.arange(band_length, dtype=jnp.int32)
    distance = query_places[:, None] - key_places[None, :]
    visible = (distance >= 0) & (distance < WINDOW_LENGTH) & (key_places[None, :] >= 0)
    grouped = query_rot.reshape(tokens, pair_heads, group_count, head_size)
    scores = (
        jnp.einsum(
            "qhgd,shd->hgqs",
            grouped,
            keys_band.reshape(band_length, pair_heads, head_size),
            preferred_element_type=jnp.float32,
        )
        * scale_factor
    )
    scores = jnp.where(visible, scores, -1e30)
    row_max = jnp.max(scores, axis=-1, keepdims=True)
    exponent = jnp.exp(scores - row_max)
    weights = (exponent / jnp.sum(exponent, axis=-1, keepdims=True)).astype(jnp.bfloat16)
    attended = jnp.einsum(
        "hgqs,shd->qhgd",
        weights,
        values_band.reshape(band_length, pair_heads, head_size),
        preferred_element_type=jnp.float32,
    )
    return attended.reshape(tokens, -1).astype(jnp.bfloat16)


def on_device_sharing(
    stream_in,
    in_gain,
    query_weight,
    key_matrix,
    value_matrix,
    query_gain,
    key_norm_gain,
    output_weight,
    post_gain,
):
    group = lax.axis_index("groups")
    head_size = query_gain.shape[0]
    rows = lax.axis_size("row")

    def own_columns(w):
        width = w.shape[1] // 2
        return lax.dynamic_slice_in_dim(w, group * width, width, axis=1)

    def halves(w):
        own = rows_gathered(own_columns(w))
        other = swapped(own)
        full = rows * w.shape[0]
        return (own.reshape(full, -1), other.reshape(full, -1))

    key_halves = halves(key_matrix)
    token_rows = lax.all_gather(stream_in, ("col", "sub"), axis=1, tiled=True)
    value_halves = halves(value_matrix)
    query_halves = halves(query_weight)
    depth = output_weight.shape[0]
    half, quarter = (depth // 2, depth // 4)
    out_own = rows_gathered(lax.dynamic_slice_in_dim(output_weight, group * half, half, axis=0))
    out_peer = swapped(out_own[:, :quarter])
    out_direct = rows_gathered(
        lax.dynamic_slice_in_dim(output_weight, (1 - group) * half + quarter, quarter, axis=0)
    )
    tokens = token_rows.shape[0]
    normed = root_mean_scale(token_rows.astype(jnp.float32), in_gain).astype(jnp.bfloat16)

    def add_panel(panel):
        return jnp.dot(normed, panel, preferred_element_type=jnp.float32)

    scale_factor = float(MODEL_WIDTH // QUERY_HEAD_COUNT) ** (-0.5)
    row_index = lax.axis_index("row")
    places = (row_index * tokens + jnp.arange(tokens, dtype=jnp.int32)).astype(jnp.float32)

    def rotated(projected, gain):
        heads = projected.reshape(tokens, -1, head_size)
        return apply_rotary(root_mean_scale(heads, gain), places).astype(jnp.bfloat16)

    attended = []
    for i in range(2):
        keys_flat = rotated(add_panel(key_halves[i]), key_norm_gain).reshape(tokens, -1)
        values_flat = add_panel(value_halves[i]).astype(jnp.bfloat16)
        query_rot = rotated(add_panel(query_halves[i]), query_gain)
        heads_out = attend(query_rot, keys_flat, values_flat, row_index, head_size, scale_factor)
        attended.append(lax.all_gather(heads_out, ("col", "sub"), axis=1, tiled=True))
    own_rows, other_rows = attended
    blocks = other_rows.reshape(tokens, -1, half)
    branch = (
        jnp.dot(
            own_rows, out_own.reshape(-1, out_own.shape[-1]), preferred_element_type=jnp.float32
        )
        + jnp.dot(
            blocks[:, :, quarter:].reshape(tokens, -1),
            out_direct.reshape(-1, out_direct.shape[-1]),
            preferred_element_type=jnp.float32,
        )
        + jnp.dot(
            blocks[:, :, :quarter].reshape(tokens, -1),
            out_peer.reshape(-1, out_peer.shape[-1]),
            preferred_element_type=jnp.float32,
        )
    )
    squares = lax.psum(jnp.sum(branch * branch, axis=-1), ("col", "sub"))
    scaled = branch * lax.rsqrt(squares[:, None] / MODEL_WIDTH + EPSILON) * post_gain
    return (stream_in.astype(jnp.float32) + scaled).astype(jnp.bfloat16)


def on_device_any(*operands):
    head_size = operands[5].shape[0]
    pair_heads = operands[3].shape[1] // head_size
    blocks_agree = lax.axis_size("row") == lax.axis_size("col") * lax.axis_size("sub")
    if lax.axis_size("groups") == 2 and pair_heads % 2 == 0 and blocks_agree:
        return on_device_sharing(*operands)
    return on_device(*operands)


def solution(mesh):
    placed = (
        P(("groups", "row"), ("col", "sub")),
        P(),
        P("row", ("col", "sub")),
        P("row", ("col", "sub")),
        P("row", ("col", "sub")),
        P(),
        P(),
        P("row", ("col", "sub")),
        P(("col", "sub")),
    )
    return jax.shard_map(
        on_device_any,
        mesh=mesh,
        in_specs=placed,
        out_specs=P(("groups", "row"), ("col", "sub")),
        check_vma=False,
    )
```

profile of v0, /device:TPU:22, one launch (start us, length us, event | category | flops | bytes accessed | tf_op | source)
XLA Modules:
  0.0 608.8 jit_solution(1578314653373979051)
XLA Ops:
  6.5 2.1 constant_dynamic-slice_fusion.3
  8.8 2.5 constant_dynamic-slice_fusion.2
  11.3 2.0 constant_dynamic-slice_fusion.4
  13.4 0.5 all-gather.14.cloned.1.call-update
  14.0 1.3 constant_dynamic-slice_fusion.1
  15.3 50.3 %all-gather.22.cloned.1.call-done = bf16[5376,256]{1,0:T(8,128)(2,1)} async-done(((bf16[1344,256]{1,0:T(8,128)(2,1)}), bf16[5376,256]{1,0:T(8,128)(2,1)}) %all-gather.22.cloned.1.call-update) | async-done | bytes 2752528 | tf_op jit(solution)/shard_map/all_gather | solution.py:128
  65.6 0.5 collective-permute-start.7
  66.2 1.0 constant_dynamic-slice_fusion
  67.3 0.5 multiply_cosine_fusion
  67.8 100.0 %all-gather.24.cloned.1.call-done = bf16[5376,512]{1,0:T(8,128)(2,1)} async-done(((bf16[1344,512]{1,0:T(8,128)(2,1)}), bf16[5376,512]{1,0:T(8,128)(2,1)}) %all-gather.24.cloned.1.call-update) | async-done | bytes 5505040 | tf_op jit(solution)/shard_map/all_gather | solution.py:128
  167.9 0.6 collective-permute-start.10
  168.4 1.9 fusion.25
  170.3 3.3 copy.28
  173.6 51.5 %all-gather.20.cloned.1.call-done = bf16[5376,256]{1,0:T(8,128)(2,1)} async-done(((bf16[1344,256]{1,0:T(8,128)(2,1)}), bf16[5376,256]{1,0:T(8,128)(2,1)}) %all-gather.20.cloned.1.call-update) | async-done | bytes 2752528 | tf_op jit(solution)/shard_map/all_gather | solution.py:128
  225.1 0.6 collective-permute-start.4
  225.7 4.6 copy.37
  230.3 37.3 %all-gather.14.cloned.1.call-done = bf16[512,5376]{0,1:T(8,128)(2,1)} async-done(((bf16[512,1344]{0,1:T(8,128)(2,1)}), bf16[512,5376]{0,1:T(8,128)(2,1)}) %all-gather.14.cloned.1.call-update) | async-done | bytes 5505040 | tf_op jit(solution)/shard_map/all_gather | solution.py:198
  267.5 3.9 fusion.2
  271.7 3.7 multiply_reduce_fusion.3
  275.4 1.9 multiply_reduce_fusion.4
  277.6 0.8 multiply_subtract_fusion.1
  278.4 0.7 maximum_convert_fusion.1
  279.1 1.3 collective-permute-start.8
  280.4 3.4 collective-permute-start.9
  283.8 63.6 %collective-permute-done.4 = bf16[4,1344,256]{2,1,0:T(8,128)(2,1)} collective-permute-done((bf16[4,1344,256]{2,1,0:T(8,128)(2,1)}, bf16[4,1344,256]{2,1,0:T(8,128)(2,1)}, u32[]{:S(2)}, u32[]{:S(2)}) %collective-permute-start.4) | collective-permute-done | bytes 2752544 | tf_op jit(solution)/shard_map/ppermute | solution.py:124
  347.4 4.5 convolution_convert_fusion
  351.9 1.3 collective-permute-start.5
  353.2 3.1 collective-permute-start.6
  356.3 8.2 %copy.30 = bf16[512,5376]{1,0:T(8,128)(2,1)} copy(bf16[512,5376]{0,1:T(8,128)(2,1)} %bitcast.135) | data formatting | bytes 11010048 | tf_op jit(solution)/shard_map/dot_general | solution.py:212
  364.6 8.3 %multiply_reduce_fusion.2 = (f32[512,4]{0,1:T(4,128)S(1)}, f32[512,4,128]{0,2,1:T(8,128)}) fusion(bf16[4,128,5376]{2,1,0:T(8,128)(2,1)} %bitcast.137, f32[5376]{0:T(1024)S(1)} %copy-done.11, f32[512]{0:T(512)S(1)} %add_rsqrt_fusion.5, bf16[512,5376]{0,1:T(8,128)(2,1)} %all-gather.14.cloned.1.call-done), kind=kOutput, calls=%fused_computation.52 | convolution fusion | flops 2830104576 | bytes 12090368 | tf_op jit(solution)/shard_map/dot_general | solution.py:212
  372.9 23.0 %collective-permute-done.6 = bf16[512,256]{1,0:T(8,128)(2,1)S(1)} collective-permute-done((bf16[512,256]{1,0:T(8,128)(2,1)S(1)}, bf16[512,256]{1,0:T(8,128)(2,1)S(1)}, u32[]{:S(2)}, u32[]{:S(2)}) %collective-permute-start.6) | collective-permute-done | bytes 262176 | tf_op jit(solution)/shard_map/ppermute | solution.py:15
  395.9 1.2 copy.68
  397.1 8.1 %copy.39 = bf16[512,5376]{1,0:T(8,128)(2,1)} copy(bf16[512,5376]{0,1:T(8,128)(2,1)} %bitcast.35) | data formatting | bytes 11010048 | tf_op jit(solution)/shard_map/dot_general | solution.py:212
  405.1 7.4 %multiply_reduce_fusion.1 = (f32[512,4]{0,1:T(4,128)S(1)}, f32[512,4,128]{0,2,1:T(8,128)S(1)}) fusion(bf16[4,128,5376]{2,1,0:T(8,128)(2,1)} %bitcast.136, f32[5376]{0:T(1024)S(1)} %copy-done.11, f32[512]{0:T(512)S(1)} %add_rsqrt_fusion.5, bf16[512,5376]{0,1:T(8,128)(2,1)} %all-gather.14.cloned.1.call-done), kind=kOutput, calls=%fused_computation.50 | convolution fusion | flops 2830104576 | bytes 12090368 | tf_op jit(solution)/shard_map/dot_general | solution.py:212
  412.6 0.5 multiply_multiply_fusion.1
  413.1 0.3 subtract_convert_fusion.1
  413.4 0.3 copy.41
  413.7 0.3 copy.42
  414.0 11.0 %fusion.55 = (f32[2,2,512]{2,1,0:T(2,128)S(1)}, f32[2,2,512,1536]{2,3,1,0:T(8,128)}) fusion(pred[512,1536]{0,1:T(8,128)(4,1)} %fusion.25, bf16[512,2,128]{0,2,1:T(8,128)(2,1)} %maximum_convert_fusion.1, bf16[512,2,128]{0,2,1:T(8,128)(2,1)} %bitcast.30, bf16[512,2,128]{0,2,1:T(8,128)(2,1)} %bitcast.29, bf16[512,2,2,64]{3,0,2,1:T(8,128)(2,1)S(1)} %copy.42, ...), kind=kOutput, calls=%fused_computation.101 | convolution fusion | flops 821298688 | bytes 14688256 | tf_op jit(solution)/shard_map/sub | solution.py:161
  425.0 6.4 %fusion.30 = bf16[2,128,2,512]{3,1,2,0:T(8,128)(2,1)} fusion(bf16[1536,2,128,1]{0,2,3,1:T(8,128)(2,1)S(1)} %bitcast.147, f32[2,2,512,1536]{2,3,1,0:T(8,128)} %get-tuple-element.32, f32[2,2,512]{2,1,0:T(2,128)S(1)} %get-tuple-element.31), kind=kOutput, calls=%fused_computation.43 | convolution fusion | flops 811859968 | bytes 13901824 | tf_op jit(solution)/shard_map/hgqs,shd->qhgd/dot_general | solution.py:163
  431.7 6.0 convolution_convert_fusion.1
  437.7 1.3 collective-permute-start
  439.0 1.9 collective-permute-start.1
  441.0 0.7 maximum_convert_fusion
  441.7 1.3 collective-permute-start.2
  443.0 1.9 collective-permute-start.3
  444.9 10.4 %collective-permute-done = bf16[512,256]{1,0:T(8,128)(2,1)S(1)} collective-permute-done((bf16[512,256]{1,0:T(8,128)(2,1)S(1)}, bf16[512,256]{1,0:T(8,128)(2,1)S(1)}, u32[]{:S(2)}, u32[]{:S(2)}) %collective-permute-start) | collective-permute-done | bytes 262176 | tf_op jit(solution)/shard_map/ppermute | solution.py:15
  455.3 25.9 %collective-permute-done.1 = bf16[512,256]{1,0:T(8,128)(2,1)S(1)} collective-permute-done((bf16[512,256]{1,0:T(8,128)(2,1)S(1)}, bf16[512,256]{1,0:T(8,128)(2,1)S(1)}, u32[]{:S(2)}, u32[]{:S(2)}) %collective-permute-start.1) | collective-permute-done | bytes 262176 | tf_op jit(solution)/shard_map/ppermute | solution.py:15
  481.3 0.3 copy.63
  481.9 0.3 copy.33
  482.2 10.9 %collective-permute-done.3 = bf16[512,256]{0,1:T(8,128)(2,1)} collective-permute-done((bf16[512,256]{0,1:T(8,128)(2,1)}, bf16[512,256]{0,1:T(8,128)(2,1)}, u32[]{:S(2)}, u32[]{:S(2)}) %collective-permute-start.3) | collective-permute-done | bytes 262176 | tf_op jit(solution)/shard_map/ppermute | solution.py:15
  493.0 10.7 %fusion.56 = (f32[2,2,512]{2,1,0:T(2,128)S(1)}, f32[2,2,512,1536]{2,3,1,0:T(8,128)}) fusion(pred[512,1536]{0,1:T(8,128)(4,1)S(1)} %copy-done.4, bf16[512,2,128]{0,2,1:T(8,128)(2,1)} %maximum_convert_fusion, bf16[512,2,128]{0,2,1:T(8,128)(2,1)} %bitcast.8, bf16[512,2,128]{0,2,1:T(8,128)(2,1)} %bitcast.7, bf16[512,2,2,64]{3,0,2,1:T(8,128)(2,1)S(1)} %copy.33, ...), kind=kOutput, calls=%fused_computation.102 | convolution fusion | flops 821298688 | bytes 14688256 | tf_op jit(solution)/shard_map/sub | solution.py:161
  503.7 6.4 %fusion.31 = bf16[2,128,2,512]{3,1,2,0:T(8,128)(2,1)} fusion(bf16[1536,2,128,1]{0,2,3,1:T(8,128)(2,1)S(1)} %bitcast.148, f32[2,2,512,1536]{2,3,1,0:T(8,128)} %get-tuple-element.34, f32[2,2,512]{2,1,0:T(2,128)S(1)} %get-tuple-element.33), kind=kOutput, calls=%fused_computation.44 | convolution fusion | flops 811859968 | bytes 13901824 | tf_op jit(solution)/shard_map/hgqs,shd->qhgd/dot_general | solution.py:163
  510.2 8.6 %copy.50 = bf16[2048,1344]{1,0:T(8,128)(2,1)} copy(bf16[2048,1344]{0,1:T(8,128)(2,1)} %all-gather.26.cloned.1.call-done) | data formatting | bytes 11010048 | tf_op jit(solution)/shard_map/all_gather | solution.py:128
  518.7 3.7 slice.53
  522.4 3.1 copy.75
  525.5 0.6 collective-permute-start.11
  526.1 4.5 copy.47
  530.7 5.4 convolution_bitcast_fusion.1
  536.0 7.3 %convolution_add_fusion = f32[512,1344]{0,1:T(8,128)S(1)} fusion(f32[512,1344]{0,1:T(8,128)} %convolution_bitcast_fusion.1, bf16[2048,1344]{0,1:T(8,128)(2,1)} %all-gather.26.cloned.1.call-done, bf16[512,2048]{0,1:T(8,128)(2,1)} %all-gather.16.cloned.1.call-done), kind=kOutput, calls=%fused_computation.33 | convolution fusion | flops 2819260416 | bytes 13107200 | tf_op jit(solution)/shard_map/dot_general | solution.py:232
  543.3 43.6 %collective-permute-done.11 = bf16[4,256,1344]{1,2,0:T(8,128)(2,1)} collective-permute-done((bf16[4,256,1344]{1,2,0:T(8,128)(2,1)S(1)}, bf16[4,256,1344]{1,2,0:T(8,128)(2,1)}, u32[]{:S(2)}, u32[]{:S(2)}) %collective-permute-start.11) | collective-permute-done | bytes 2752544 | tf_op jit(solution)/shard_map/ppermute | solution.py:124
  586.9 5.1 multiply_reduce_fusion
  592.1 5.9 psum.7
  598.0 3.7 add_convert_fusion
  (64 shorter events, 1.6 us)
Async XLA Ops:
  6.5 7.5 %copy-start = (bf16[1024,1344]{0,1:T(8,128)(2,1)S(1)}, bf16[1024,1344]{0,1:T(8,128)(2,1)}, u32[]{:S(2)}) copy-start(bf16[1024,1344]{0,1:T(8,128)(2,1)} %param.16) | copy-start | bytes 8257540
  6.5 59.1 %all-gather.22.cloned.1.call-start = ((), (), s32[]{:S(2)}) async-start(), calls=%async_computation.4 | async-start | bytes 3440640 | tf_op jit(solution)/shard_map/all_gather | solution.py:128
  8.7 159.1 %all-gather.24.cloned.1.call-start = ((), (), s32[]{:S(2)}) async-start(), calls=%async_computation.5 | async-start | bytes 6881280 | tf_op jit(solution)/shard_map/all_gather | solution.py:128
  11.3 213.8 %all-gather.20.cloned.1.call-start = ((), (), s32[]{:S(2)}) async-start(), calls=%async_computation.3 | async-start | bytes 3440640 | tf_op jit(solution)/shard_map/all_gather | solution.py:128
  13.4 254.2 %all-gather.14.cloned.1.call-start = ((), (), s32[]{:S(2)}) async-start(), calls=%async_computation | async-start | bytes 6881280 | tf_op jit(solution)/shard_map/all_gather | solution.py:198
  14.0 496.2 %all-gather.26.cloned.1.call-start = ((), (), s32[]{:S(2)}) async-start(), calls=%async_computation.6 | async-start | bytes 6881280 | tf_op jit(solution)/shard_map/all_gather | solution.py:128
  15.3 510.8 %all-gather.28.cloned.1.call-start = ((), (), s32[]{:S(2)}) async-start(), calls=%async_computation.7 | async-start | bytes 3440640 | tf_op jit(solution)/shard_map/all_gather | solution.py:128
  65.6 160.1 %collective-permute-start.7 = (bf16[4,1344,256]{2,1,0:T(8,128)(2,1)}, bf16[4,1344,256]{2,1,0:T(8,128)(2,1)}, u32[]{:S(2)}, u32[]{:S(2)}) collective-permute-start(bf16[4,1344,256]{2,1,0:T(8,128)(2,1)} %bitcast.139), channel_id=1, source_target_pairs={{0,16},{16,0},{1,17},{17,1},{2,18},{18,2},{3,19},{19,3},{4,20},{20... | collective-permute-start | bytes 8257544 | tf_op jit(solution)/shard_map/ppermute | solution.py:124
  67.2 463.5 %all-gather.18.cloned.1.call-start = ((), (), s32[]{:S(2)}) async-start(), calls=%async_computation.2 | async-start | bytes 2621440 | tf_op jit(solution)/shard_map/all_gather | solution.py:228
  167.9 229.2 %collective-permute-start.10 = (bf16[4,1344,512]{2,1,0:T(8,128)(2,1)}, bf16[4,1344,512]{2,1,0:T(8,128)(2,1)}, u32[]{:S(2)}, u32[]{:S(2)}) collective-permute-start(bf16[4,1344,512]{2,1,0:T(8,128)(2,1)} %bitcast.134), channel_id=1, source_target_pairs={{0,16},{16,0},{1,17},{17,1},{2,18},{18,2},{3,19},{19,3},{4,20},{20... | collective-permute-start | bytes 16515080 | tf_op jit(solution)/shard_map/ppermute | solution.py:124
  225.1 122.3 %collective-permute-start.4 = (bf16[4,1344,256]{2,1,0:T(8,128)(2,1)}, bf16[4,1344,256]{2,1,0:T(8,128)(2,1)}, u32[]{:S(2)}, u32[]{:S(2)}) collective-permute-start(bf16[4,1344,256]{2,1,0:T(8,128)(2,1)} %bitcast.151), channel_id=1, source_target_pairs={{0,16},{16,0},{1,17},{17,1},{2,18},{18,2},{3,19},{19,3},{4,20},{20... | collective-permute-start | bytes 8257544 | tf_op jit(solution)/shard_map/ppermute | solution.py:124
  225.7 45.8 %copy-start.11 = (f32[5376]{0:T(1024)S(1)}, f32[5376]{0:T(1024)}, u32[]{:S(2)}) copy-start(f32[5376]{0:T(1024)} %param.10) | copy-start | bytes 64516
  267.5 4.2 copy-start.2
  275.4 2.0 copy-start.8
  279.1 134.9 %collective-permute-start.8 = (bf16[512,256]{0,1:T(8,128)(2,1)}, bf16[512,256]{0,1:T(8,128)(2,1)}, u32[]{:S(2)}, u32[]{:S(2)}) collective-permute-start(bf16[512,256]{0,1:T(8,128)(2,1)} %bitcast.28), channel_id=1, source_target_pairs={{0,8},{4,12},{1,9},{5,13},{2,10},{6,14},{3,11},{7,15},{16,24},{20,... | collective-permute-start | bytes 786440 | tf_op jit(solution)/shard_map/ppermute | solution.py:15
  280.4 133.6 %collective-permute-start.9 = (bf16[512,256]{0,1:T(8,128)(2,1)}, bf16[512,256]{0,1:T(8,128)(2,1)}, u32[]{:S(2)}, u32[]{:S(2)}) collective-permute-start(bf16[512,256]{0,1:T(8,128)(2,1)} %bitcast.28), channel_id=1, source_target_pairs={{0,4},{4,8},{8,12},{1,5},{5,9},{9,13},{2,6},{6,10},{10,14},{3,7},{... | collective-permute-start | bytes 786440 | tf_op jit(solution)/shard_map/ppermute | solution.py:15
  351.9 21.0 %collective-permute-start.5 = (bf16[512,256]{1,0:T(8,128)(2,1)S(1)}, bf16[512,256]{1,0:T(8,128)(2,1)S(1)}, u32[]{:S(2)}, u32[]{:S(2)}) collective-permute-start(bf16[512,256]{1,0:T(8,128)(2,1)S(1)} %convolution_convert_fusion), channel_id=1, source_target_pairs={{0,8},{4,12},{1,9},{5,13},{2,10},{6,14},{3,11},{7,15},{16,24},{20,... | collective-permute-start | bytes 786440 | tf_op jit(solution)/shard_map/ppermute | solution.py:15
  353.2 42.6 %collective-permute-start.6 = (bf16[512,256]{1,0:T(8,128)(2,1)S(1)}, bf16[512,256]{1,0:T(8,128)(2,1)S(1)}, u32[]{:S(2)}, u32[]{:S(2)}) collective-permute-start(bf16[512,256]{1,0:T(8,128)(2,1)S(1)} %convolution_convert_fusion), channel_id=1, source_target_pairs={{0,4},{4,8},{8,12},{1,5},{5,9},{9,13},{2,6},{6,10},{10,14},{3,7},{... | collective-permute-start | bytes 786440 | tf_op jit(solution)/shard_map/ppermute | solution.py:15
  405.1 7.4 %copy-start.3 = (f32[512,4,128]{0,2,1:T(8,128)S(1)}, f32[512,4,128]{0,2,1:T(8,128)}, u32[]{:S(2)}) copy-start(f32[512,4,128]{0,2,1:T(8,128)} %get-tuple-element.28) | copy-start | bytes 3145732
  405.1 7.4 %copy-start.9 = (f32[128]{0:T(128)S(1)}, f32[128]{0:T(128)}, u32[]{:S(2)}) copy-start(f32[128]{0:T(128)} %param.14) | copy-start | bytes 1540
  414.0 11.0 %copy-start.5 = (bf16[1536,256]{0,1:T(8,128)(2,1)S(1)}, bf16[1536,256]{0,1:T(8,128)(2,1)}, u32[]{:S(2)}) copy-start(bf16[1536,256]{0,1:T(8,128)(2,1)} %copy.68) | copy-start | bytes 2359300
  425.0 6.7 %copy-start.12 = (f32[5376]{0:T(1024)S(1)}, f32[5376]{0:T(1024)}, u32[]{:S(2)}) copy-start(f32[5376]{0:T(1024)} %param.10) | copy-start | bytes 64516
  431.5 9.5 %copy-start.6 = (bf16[512,2,64]{0,2,1:T(8,128)(2,1)S(1)}, bf16[512,2,64]{0,2,1:T(8,128)(2,1)}, u32[]{:S(2)}) copy-start(bf16[512,2,64]{0,2,1:T(8,128)(2,1)} %get-tuple-element.10) | copy-start | bytes 393220
  431.5 61.5 %copy-start.4 = (pred[512,1536]{0,1:T(8,128)(4,1)S(1)}, pred[512,1536]{0,1:T(8,128)(4,1)}, u32[]{:S(2)}) copy-start(pred[512,1536]{0,1:T(8,128)(4,1)} %fusion.25) | copy-start | bytes 2359300
  431.5 104.5 %all-gather.16.cloned.1.call-start = ((), (), s32[]{:S(2)}) async-start(), calls=%async_computation.1 | async-start | bytes 2621440 | tf_op jit(solution)/shard_map/all_gather | solution.py:228
  437.7 17.6 %collective-permute-start = (bf16[512,256]{1,0:T(8,128)(2,1)S(1)}, bf16[512,256]{1,0:T(8,128)(2,1)S(1)}, u32[]{:S(2)}, u32[]{:S(2)}) collective-permute-start(bf16[512,256]{1,0:T(8,128)(2,1)S(1)} %convolution_convert_fusion.1), channel_id=1, source_target_pairs={{0,8},{4,12},{1,9},{5,13},{2,10},{6,14},{3,11},{7,15},{16,24},{20,... | collective-permute-start | bytes 786440 | tf_op jit(solution)/shard_map/ppermute | solution.py:15
  439.0 42.2 %collective-permute-start.1 = (bf16[512,256]{1,0:T(8,128)(2,1)S(1)}, bf16[512,256]{1,0:T(8,128)(2,1)S(1)}, u32[]{:S(2)}, u32[]{:S(2)}) collective-permute-start(bf16[512,256]{1,0:T(8,128)(2,1)S(1)} %convolution_convert_fusion.1), channel_id=1, source_target_pairs={{0,4},{4,8},{8,12},{1,5},{5,9},{9,13},{2,6},{6,10},{10,14},{3,7},{... | collective-permute-start | bytes 786440 | tf_op jit(solution)/shard_map/ppermute | solution.py:15
  441.7 40.4 %collective-permute-start.2 = (bf16[512,256]{0,1:T(8,128)(2,1)}, bf16[512,256]{0,1:T(8,128)(2,1)}, u32[]{:S(2)}, u32[]{:S(2)}) collective-permute-start(bf16[512,256]{0,1:T(8,128)(2,1)} %bitcast.6), channel_id=1, source_target_pairs={{0,8},{4,12},{1,9},{5,13},{2,10},{6,14},{3,11},{7,15},{16,24},{20,... | collective-permute-start | bytes 786440 | tf_op jit(solution)/shard_map/ppermute | solution.py:15
  443.0 50.0 %collective-permute-start.3 = (bf16[512,256]{0,1:T(8,128)(2,1)}, bf16[512,256]{0,1:T(8,128)(2,1)}, u32[]{:S(2)}, u32[]{:S(2)}) collective-permute-start(bf16[512,256]{0,1:T(8,128)(2,1)} %bitcast.6), channel_id=1, source_target_pairs={{0,4},{4,8},{8,12},{1,5},{5,9},{9,13},{2,6},{6,10},{10,14},{3,7},{... | collective-permute-start | bytes 786440 | tf_op jit(solution)/shard_map/ppermute | solution.py:15
  525.5 61.4 %collective-permute-start.11 = (bf16[4,256,1344]{1,2,0:T(8,128)(2,1)S(1)}, bf16[4,256,1344]{1,2,0:T(8,128)(2,1)}, u32[]{:S(2)}, u32[]{:S(2)}) collective-permute-start(bf16[4,256,1344]{1,2,0:T(8,128)(2,1)S(1)} %copy.75), channel_id=1, source_target_pairs={{0,16},{16,0},{1,17},{17,1},{2,18},{18,2},{3,19},{19,3},{4,20},{20... | collective-permute-start | bytes 8257544 | tf_op jit(solution)/shard_map/ppermute | solution.py:124
  536.0 50.9 %copy-start.10 = (bf16[512,2048]{0,1:T(8,128)(2,1)S(1)}, bf16[512,2048]{0,1:T(8,128)(2,1)}, u32[]{:S(2)}) copy-start(bf16[512,2048]{0,1:T(8,128)(2,1)} %all-gather.18.cloned.1.call-done) | copy-start | bytes 6291460
  543.3 54.6 %copy-start.7 = (f32[1344]{0:T(1024)S(1)}, f32[1344]{0:T(1024)}, u32[]{:S(2)}) copy-start(f32[1344]{0:T(1024)} %param.17) | copy-start | bytes 16132
  586.9 14.8 %copy-start.1 = (bf16[1024,1344]{0,1:T(8,128)(2,1)S(1)}, bf16[1024,1344]{0,1:T(8,128)(2,1)}, u32[]{:S(2)}) copy-start(bf16[1024,1344]{0,1:T(8,128)(2,1)} %param.16) | copy-start | bytes 8257540
Sparse Core Ops, SparseCore 0:
  8.9 56.6 all-gather.21
  67.2 100.6 all-gather.23
  169.4 55.6 all-gather.19
  226.5 40.9 all-gather.13
  269.0 119.5 all-gather.25
  390.0 82.8 all-gather.27
  474.4 33.1 all-gather.17
  510.3 21.6 all-gather.15
where the time goes:
time: 618 us; the launch traced here: 609 us
  waiting for transfers between devices  417 us (67%)
  matrix products  84.1 us (14%)
  local copies, waits for them, and re-layouts  55.8 us (9%)
  starting transfers between devices  18.2 us (3%)
  between operations  14.1 us (2%)
  other arithmetic  13.6 us (2%)
    all_gather x5, waiting for transfers between devices, rows_gathered(): return lax.all_gather(piece, 'row', axis=0)  202 us
    ppermute x4, waiting for transfers between devices, swapped(): return lax.ppermute(x, 'groups', [(i, count - 1 - i) for i in range(count)])  107 us
    ppermute x8, waiting for transfers between devices, shifted(): return lax.ppermute(x, axis, pairs)  70.2 us
    all_gather x1, waiting for transfers between devices, on_device_sharing(): token_rows = lax.all_gather(stream_in, ('col', 'sub'), axis=1, tiled=True)  37.3 us
    dot_general x6, matrix products, add_panel(): return jnp.dot(normed, panel, preferred_element_type=jnp.float32)  31.8 us
    dot_general x4, local copies, waits for them, and re-layouts, add_panel(): return jnp.dot(normed, panel, preferred_element_type=jnp.float32)  24.2 us
    sub x2, matrix products, attend(): exponent = jnp.exp(scores - row_max)  21.7 us
    ppermute x8, starting transfers between devices, shifted(): return lax.ppermute(x, axis, pairs)  15.5 us
  transfers between devices with their start and end apart: 20, of which 10 were waited for; matrix products, arithmetic and copies ran while one was open for 23% of the time, Pallas kernels for 0%

commit v1 on v0

--- a/solution.py
+++ b/solution.py
@@ -7,6 +7,19 @@
 QUERY_HEAD_COUNT = 32
 WINDOW_LENGTH = 1024
 EPSILON = 1e-06
+
+
+def ring_gather(shard, axis, dim):
+    ways = lax.axis_size(axis)
+    up = [(d, (d + 1) % ways) for d in range(ways)]
+    down = [(d, (d - 1) % ways) for d in range(ways)]
+    earlier, later = ([shard], [shard])
+    for _ in range(ways // 2):
+        earlier.append(lax.ppermute(earlier[-1], axis, up))
+    for _ in range((ways - 1) // 2):
+        later.append(lax.ppermute(later[-1], axis, down))
+    line = jnp.concatenate([*earlier[::-1], *later[1:]], axis=dim)
+    return jnp.roll(line, (lax.axis_index(axis) - ways // 2) * shard.shape[dim], axis=dim)
 
 
 def shifted(x, axis, by):
@@ -195,7 +208,7 @@
         return (own.reshape(full, -1), other.reshape(full, -1))
 
     key_halves = halves(key_matrix)
-    token_rows = lax.all_gather(stream_in, ("col", "sub"), axis=1, tiled=True)
+    token_rows = ring_gather(stream_in, ("col", "sub"), 1)
     value_halves = halves(value_matrix)
     query_halves = halves(query_weight)
     depth = output_weight.shape[0]

time: 618 us -> 576 us (0.932)
  waiting for transfers between devices: 417 us -> 347 us
  local copies, waits for them, and re-layouts: 55.8 us -> 72.3 us
  matrix products: 84.1 us -> 92.5 us
    all_gather x5, waiting for transfers between devices: 202 us -> 148 us  [rows_gathered(): return lax.all_gather(piece, 'row', axis=0)]
    ppermute x0 -> x3, waiting for transfers between devices: none -> 44.5 us  [the longest x2 44.5 us: ring_gather(): earlier.append(lax.ppermute(earlier[-1], axis, up))]
    ppermute x4, waiting for transfers between devices: 107 us -> 67.6 us  [swapped(): return lax.ppermute(x, 'groups', [(i, count - 1 - i) for i in range(count)])]
    all_gather x1 -> x0, waiting for transfers between devices: 37.3 us -> none  [on_device_sharing(): token_rows = lax.all_gather(stream_in, ('col', 'sub'), axis=1, tiled=True)]
    ppermute x8, waiting for transfers between devices: 70.2 us -> 86.4 us  [shifted(): return lax.ppermute(x, axis, pairs)]
    unnamed x27 -> x38, local copies, waits for them, and re-layouts: 3.39 us -> 18.1 us
    dot_general x6, matrix products: 31.8 us -> 40.2 us  [add_panel(): return jnp.dot(normed, panel, preferred_element_type=jnp.float32)]
  transfers between devices with their start and end apart: 20 -> 22, of which waited for: 10 -> 11; matrix products, arithmetic and copies ran while one was open for 23% -> 30% of each run, Pallas kernels for 0% -> 0%
where the time goes in v1:
time: 576 us; the launch traced here: 566 us
  waiting for transfers between devices  347 us (60%)
  matrix products  92.5 us (16%)
  local copies, waits for them, and re-layouts  72.3 us (13%)
  starting transfers between devices  18.9 us (3%)
  other arithmetic  15.7 us (3%)
  between operations  14.4 us (2%)
  blocking collectives  5.97 us (1%)
    all_gather x5, waiting for transfers between devices, rows_gathered(): return lax.all_gather(piece, 'row', axis=0)  148 us
    ppermute x8, waiting for transfers between devices, shifted(): return lax.ppermute(x, axis, pairs)  86.4 us
    ppermute x4, waiting for transfers between devices, swapped(): return lax.ppermute(x, 'groups', [(i, count - 1 - i) for i in range(count)])  67.6 us
    ppermute x2, waiting for transfers between devices, ring_gather(): earlier.append(lax.ppermute(earlier[-1], axis, up))  44.5 us
    dot_general x6, matrix products, add_panel(): return jnp.dot(normed, panel, preferred_element_type=jnp.float32)  40.2 us
    dot_general x4, local copies, waits for them, and re-layouts, add_panel(): return jnp.dot(normed, panel, preferred_element_type=jnp.float32)  22.9 us
    sub x2, matrix products, attend(): exponent = jnp.exp(scores - row_max)  21.7 us
    unnamed x38, local copies, waits for them, and re-layouts  18.1 us
  transfers between devices with their start and end apart: 22, of which 11 were waited for; matrix products, arithmetic and copies ran while one was open for 30% of the time, Pallas kernels for 0%

profile of v1, /device:TPU:22, one launch (start us, length us, event | category | flops | bytes accessed | tf_op | source)
XLA Modules:
  0.0 566.5 jit_solution(2977495785025421930)
XLA Ops:
  6.5 2.2 constant_dynamic-slice_fusion.4
  8.8 2.0 constant_dynamic-slice_fusion.3
  10.9 2.5 constant_dynamic-slice_fusion.2
  13.4 1.2 constant_dynamic-slice_fusion.1
  14.8 1.7 collective-permute-start.2
  16.6 30.2 %collective-permute-done = bf16[512,1344]{0,1:T(8,128)(2,1)} collective-permute-done((bf16[512,1344]{0,1:T(8,128)(2,1)}, bf16[512,1344]{0,1:T(8,128)(2,1)}, u32[]{:S(2)}, u32[]{:S(2)}) %collective-permute-start) | collective-permute-done | bytes 1376288 | tf_op jit(solution)/shard_map/ppermute | solution.py:18
  46.8 1.0 constant_dynamic-slice_fusion
  48.5 2.0 fusion.25
  50.5 14.3 %collective-permute-done.1 = bf16[512,1344]{0,1:T(8,128)(2,1)} collective-permute-done((bf16[512,1344]{0,1:T(8,128)(2,1)}, bf16[512,1344]{0,1:T(8,128)(2,1)}, u32[]{:S(2)}, u32[]{:S(2)}) %collective-permute-start.1) | collective-permute-done | bytes 1376288 | tf_op jit(solution)/shard_map/ppermute | solution.py:18
  64.8 2.5 constant_dynamic-update-slice_fusion.7
  67.4 2.5 constant_dynamic-update-slice_fusion.6
  70.4 1.2 constant_dynamic-update-slice_fusion.5
  71.6 2.5 constant_dynamic-update-slice_fusion.4
  74.1 48.8 %all-gather.19.cloned.1.call-done = bf16[5376,256]{1,0:T(8,128)(2,1)} async-done(((bf16[1344,256]{1,0:T(8,128)(2,1)}), bf16[5376,256]{1,0:T(8,128)(2,1)}) %all-gather.19.cloned.1.call-update) | async-done | bytes 2752528 | tf_op jit(solution)/shard_map/all_gather | solution.py:141
  123.4 2.5 constant_dynamic-update-slice_fusion.3
  125.9 99.2 %all-gather.21.cloned.1.call-done = bf16[5376,512]{1,0:T(8,128)(2,1)} async-done(((bf16[1344,512]{1,0:T(8,128)(2,1)}), bf16[5376,512]{1,0:T(8,128)(2,1)}) %all-gather.21.cloned.1.call-update) | async-done | bytes 5505040 | tf_op jit(solution)/shard_map/all_gather | solution.py:141
  225.7 2.5 constant_dynamic-update-slice_fusion.2
  228.2 1.2 constant_dynamic-update-slice_fusion.1
  229.4 2.7 constant_dynamic-update-slice_fusion
  232.1 4.9 fusion.2
  237.1 2.9 copy.28
  240.0 5.8 %multiply_reduce_fusion.4 = (f32[512,2]{0,1:T(2,128)S(1)}, f32[512,2,128]{0,2,1:T(8,128)S(1)}) fusion(bf16[2,128,5376]{2,1,0:T(8,128)(2,1)} %bitcast.142, f32[5376]{0:T(1024)} %param.10, f32[512]{0:T(512)S(1)} %add_rsqrt_fusion.5, bf16[512,10752]{0,1:T(8,128)(2,1)} %constant_dynamic-update-slice_fusion, s32[]{:T(128)S(6)} %select_n.32), kind=kOutput, calls=%fused_computation.68 | convolution fusion | flops 1420557312 | bytes 8812548 | tf_op jit(solution)/shard_map/dot_general | solution.py:225
  245.8 7.1 %convolution_convert_fusion = bf16[512,256]{1,0:T(8,128)(2,1)} fusion(bf16[5376,256]{1,0:T(8,128)(2,1)} %bitcast.19, f32[5376]{0:T(1024)S(1)} %copy-done.12, f32[512]{0:T(512)S(1)} %add_rsqrt_fusion.5, bf16[512,10752]{0,1:T(8,128)(2,1)} %constant_dynamic-update-slice_fusion, s32[]{:T(128)S(6)} %select_n.32), kind=kOutput, calls=%fused_computation.45 | convolution fusion | flops 1420427264 | bytes 8543236 | tf_op jit(solution)/shard_map/dot_general | solution.py:225
  252.9 1.3 collective-permute-start.8
  254.2 2.5 collective-permute-start.9
  256.8 3.3 copy.37
  260.1 4.9 multiply_reduce_fusion.3
  265.3 0.8 multiply_subtract_fusion.1
  266.1 0.7 maximum_convert_fusion.1
  266.8 1.3 collective-permute-start.11
  268.1 1.9 collective-permute-start.12
  270.0 0.8 collective-permute-done.8
  270.8 32.0 %collective-permute-done.9 = bf16[512,256]{1,0:T(8,128)(2,1)} collective-permute-done((bf16[512,256]{1,0:T(8,128)(2,1)}, bf16[512,256]{1,0:T(8,128)(2,1)}, u32[]{:S(2)}, u32[]{:S(2)}) %collective-permute-start.9) | collective-permute-done | bytes 262176 | tf_op jit(solution)/shard_map/ppermute | solution.py:28
  302.9 1.2 pad_maximum_fusion.1
  304.0 1.2 copy.68
  305.2 8.4 %copy.30 = bf16[512,5376]{1,0:T(8,128)(2,1)} copy(bf16[512,5376]{0,1:T(8,128)(2,1)} %bitcast.135) | data formatting | bytes 11010048 | tf_op jit(solution)/shard_map/dot_general | solution.py:225
  313.6 8.5 %multiply_reduce_fusion.2 = (f32[512,4]{0,1:T(4,128)S(1)}, f32[512,4,128]{0,2,1:T(8,128)}) fusion(bf16[4,128,5376]{2,1,0:T(8,128)(2,1)} %bitcast.137, f32[5376]{0:T(1024)S(1)} %copy-done.13, f32[512]{0:T(512)S(1)} %add_rsqrt_fusion.5, bf16[512,10752]{0,1:T(8,128)(2,1)} %constant_dynamic-update-slice_fusion, s32[]{:T(128)S(6)} %select_n.32), kind=kOutput, calls=%fused_computation.52 | convolution fusion | flops 2830104576 | bytes 12090372 | tf_op jit(solution)/shard_map/dot_general | solution.py:225
  322.1 23.6 %collective-permute-done.13 = bf16[4,1344,512]{2,1,0:T(8,128)(2,1)} collective-permute-done((bf16[4,1344,512]{2,1,0:T(8,128)(2,1)}, bf16[4,1344,512]{2,1,0:T(8,128)(2,1)}, u32[]{:S(2)}, u32[]{:S(2)}) %collective-permute-start.13) | collective-permute-done | bytes 5505056 | tf_op jit(solution)/shard_map/ppermute | solution.py:137
  345.7 8.3 %copy.39 = bf16[512,5376]{1,0:T(8,128)(2,1)} copy(bf16[512,5376]{0,1:T(8,128)(2,1)} %bitcast.35) | data formatting | bytes 11010048 | tf_op jit(solution)/shard_map/dot_general | solution.py:225
  354.0 7.5 %multiply_reduce_fusion.1 = (f32[512,4]{0,1:T(4,128)S(1)}, f32[512,4,128]{0,2,1:T(8,128)S(1)}) fusion(bf16[4,128,5376]{2,1,0:T(8,128)(2,1)} %bitcast.136, f32[5376]{0:T(1024)S(1)} %copy-done.13, f32[512]{0:T(512)S(1)} %add_rsqrt_fusion.5, bf16[512,10752]{0,1:T(8,128)(2,1)} %constant_dynamic-update-slice_fusion, s32[]{:T(128)S(6)} %select_n.32), kind=kOutput, calls=%fused_computation.50 | convolution fusion | flops 2830104576 | bytes 12090372 | tf_op jit(solution)/shard_map/dot_general | solution.py:225
  363.0 11.0 %fusion.55 = (f32[2,2,512]{2,1,0:T(2,128)S(1)}, f32[2,2,512,1536]{2,3,1,0:T(8,128)}) fusion(pred[512,1536]{0,1:T(8,128)(4,1)} %fusion.25, bf16[512,2,128]{0,2,1:T(8,128)(2,1)} %maximum_convert_fusion.1, bf16[512,2,128]{0,2,1:T(8,128)(2,1)} %bitcast.30, bf16[512,2,128]{0,2,1:T(8,128)(2,1)} %bitcast.29, bf16[512,2,2,64]{3,0,2,1:T(8,128)(2,1)S(1)} %copy.42, ...), kind=kOutput, calls=%fused_computation.109 | convolution fusion | flops 821298688 | bytes 14688256 | tf_op jit(solution)/shard_map/sub | solution.py:174
  374.0 6.4 %fusion.30 = bf16[2,128,2,512]{3,1,2,0:T(8,128)(2,1)} fusion(bf16[1536,2,128,1]{0,2,3,1:T(8,128)(2,1)S(1)} %bitcast.147, f32[2,2,512,1536]{2,3,1,0:T(8,128)} %get-tuple-element.32, f32[2,2,512]{2,1,0:T(2,128)S(1)} %get-tuple-element.31), kind=kOutput, calls=%fused_computation.43 | convolution fusion | flops 811859968 | bytes 13901824 | tf_op jit(solution)/shard_map/hgqs,shd->qhgd/dot_general | solution.py:176
  380.7 6.4 %convolution_convert_fusion.1 = bf16[512,256]{1,0:T(8,128)(2,1)S(1)} fusion(bf16[5376,256]{1,0:T(8,128)(2,1)} %all-gather.17.cloned.1.call-done, f32[5376]{0:T(1024)S(1)} %copy-done.14, f32[512]{0:T(512)S(1)} %add_rsqrt_fusion.5, bf16[512,10752]{0,1:T(8,128)(2,1)} %constant_dynamic-update-slice_fusion, s32[]{:T(128)S(6)} %select_n.32), kind=kOutput, calls=%fused_computation.46 | convolution fusion | flops 1420427264 | bytes 8543236 | tf_op jit(solution)/shard_map/dot_general | solution.py:225
  387.1 1.3 collective-permute-start.3
  388.4 2.8 collective-permute-start.4
  391.2 0.7 maximum_convert_fusion
  392.0 1.3 collective-permute-start.5
  393.2 1.9 collective-permute-start.6
  395.2 9.5 %collective-permute-done.3 = bf16[512,256]{1,0:T(8,128)(2,1)S(1)} collective-permute-done((bf16[512,256]{1,0:T(8,128)(2,1)S(1)}, bf16[512,256]{1,0:T(8,128)(2,1)S(1)}, u32[]{:S(2)}, u32[]{:S(2)}) %collective-permute-start.3) | collective-permute-done | bytes 262176 | tf_op jit(solution)/shard_map/ppermute | solution.py:28
  404.6 30.4 %collective-permute-done.4 = bf16[512,256]{1,0:T(8,128)(2,1)S(1)} collective-permute-done((bf16[512,256]{1,0:T(8,128)(2,1)S(1)}, bf16[512,256]{1,0:T(8,128)(2,1)S(1)}, u32[]{:S(2)}, u32[]{:S(2)}) %collective-permute-start.4) | collective-permute-done | bytes 262176 | tf_op jit(solution)/shard_map/ppermute | solution.py:28
  436.0 13.8 %collective-permute-done.6 = bf16[512,256]{0,1:T(8,128)(2,1)} collective-permute-done((bf16[512,256]{0,1:T(8,128)(2,1)}, bf16[512,256]{0,1:T(8,128)(2,1)}, u32[]{:S(2)}, u32[]{:S(2)}) %collective-permute-start.6) | collective-permute-done | bytes 262176 | tf_op jit(solution)/shard_map/ppermute | solution.py:28
  449.7 10.7 %fusion.56 = (f32[2,2,512]{2,1,0:T(2,128)S(1)}, f32[2,2,512,1536]{2,3,1,0:T(8,128)}) fusion(pred[512,1536]{0,1:T(8,128)(4,1)S(1)} %copy-done.5, bf16[512,2,128]{0,2,1:T(8,128)(2,1)} %maximum_convert_fusion, bf16[512,2,128]{0,2,1:T(8,128)(2,1)} %bitcast.8, bf16[512,2,128]{0,2,1:T(8,128)(2,1)} %bitcast.7, bf16[512,2,2,64]{3,0,2,1:T(8,128)(2,1)S(1)} %copy.33, ...), kind=kOutput, calls=%fused_computation.110 | convolution fusion | flops 821298688 | bytes 14688256 | tf_op jit(solution)/shard_map/sub | solution.py:174
  460.4 6.5 %fusion.31 = bf16[2,128,2,512]{3,1,2,0:T(8,128)(2,1)} fusion(bf16[1536,2,128,1]{0,2,3,1:T(8,128)(2,1)S(1)} %bitcast.148, f32[2,2,512,1536]{2,3,1,0:T(8,128)} %get-tuple-element.34, f32[2,2,512]{2,1,0:T(2,128)S(1)} %get-tuple-element.33), kind=kOutput, calls=%fused_computation.44 | convolution fusion | flops 811859968 | bytes 13901824 | tf_op jit(solution)/shard_map/hgqs,shd->qhgd/dot_general | solution.py:176
  466.9 8.6 %copy.50 = bf16[2048,1344]{1,0:T(8,128)(2,1)} copy(bf16[2048,1344]{0,1:T(8,128)(2,1)} %all-gather.23.cloned.1.call-done) | data formatting | bytes 11010048 | tf_op jit(solution)/shard_map/all_gather | solution.py:141
  475.5 4.0 slice.53
  479.5 3.1 copy.75
  482.6 0.6 collective-permute-start.14
  483.2 4.5 copy.47
  487.7 5.4 convolution_bitcast_fusion.1
  493.1 7.3 %convolution_add_fusion = f32[512,1344]{0,1:T(8,128)S(1)} fusion(f32[512,1344]{0,1:T(8,128)} %convolution_bitcast_fusion.1, bf16[2048,1344]{0,1:T(8,128)(2,1)} %all-gather.23.cloned.1.call-done, bf16[512,2048]{0,1:T(8,128)(2,1)} %all-gather.13.cloned.1.call-done), kind=kOutput, calls=%fused_computation.33 | convolution fusion | flops 2819260416 | bytes 13107200 | tf_op jit(solution)/shard_map/dot_general | solution.py:245
  500.4 44.0 %collective-permute-done.14 = bf16[4,256,1344]{1,2,0:T(8,128)(2,1)} collective-permute-done((bf16[4,256,1344]{1,2,0:T(8,128)(2,1)S(1)}, bf16[4,256,1344]{1,2,0:T(8,128)(2,1)}, u32[]{:S(2)}, u32[]{:S(2)}) %collective-permute-start.14) | collective-permute-done | bytes 2752544 | tf_op jit(solution)/shard_map/ppermute | solution.py:137
  544.4 5.1 multiply_reduce_fusion
  549.5 6.0 %psum.7 = f32[512]{0:T(512)S(1)} all-reduce(f32[512]{0:T(512)S(1)} %get-tuple-element.35), channel_id=1, replica_groups=mesh['groups'=2,'row'=4,'col'=2,'sub'=2] {'col','sub'}, use_global_device_ids=true, to_apply=%region_10.11 | all-reduce | flops 512 | bytes 4096 | tf_op jit(solution)/shard_map/psum | solution.py:259
  555.5 3.7 add_convert_fusion
  (79 shorter events, 5.4 us)
Async XLA Ops:
  6.5 6.9 %copy-start = (bf16[1024,1344]{0,1:T(8,128)(2,1)S(1)}, bf16[1024,1344]{0,1:T(8,128)(2,1)}, u32[]{:S(2)}) copy-start(bf16[1024,1344]{0,1:T(8,128)(2,1)} %param.16) | copy-start | bytes 8257540
  6.5 63.3 %all-gather.17.cloned.1.call-start = ((), (), s32[]{:S(2)}) async-start(), calls=%async_computation.2 | async-start | bytes 3440640 | tf_op jit(solution)/shard_map/all_gather | solution.py:141
  8.7 114.1 %all-gather.19.cloned.1.call-start = ((), (), s32[]{:S(2)}) async-start(), calls=%async_computation.3 | async-start | bytes 3440640 | tf_op jit(solution)/shard_map/all_gather | solution.py:141
  10.8 214.3 %all-gather.21.cloned.1.call-start = ((), (), s32[]{:S(2)}) async-start(), calls=%async_computation.4 | async-start | bytes 6881280 | tf_op jit(solution)/shard_map/all_gather | solution.py:141
  13.4 453.5 %all-gather.23.cloned.1.call-start = ((), (), s32[]{:S(2)}) async-start(), calls=%async_computation.5 | async-start | bytes 6881280 | tf_op jit(solution)/shard_map/all_gather | solution.py:141
  14.7 468.5 %all-gather.25.cloned.1.call-start = ((), (), s32[]{:S(2)}) async-start(), calls=%async_computation.6 | async-start | bytes 3440640 | tf_op jit(solution)/shard_map/all_gather | solution.py:141
  14.8 32.0 %collective-permute-start = (bf16[512,1344]{0,1:T(8,128)(2,1)}, bf16[512,1344]{0,1:T(8,128)(2,1)}, u32[]{:S(2)}, u32[]{:S(2)}) collective-permute-start(bf16[512,1344]{0,1:T(8,128)(2,1)} %param.9), channel_id=1, source_target_pairs={{0,1},{1,2},{2,3},{3,0},{4,5},{5,6},{6,7},{7,4},{8,9},{9,10},{10,1... | collective-permute-start | bytes 4128776 | tf_op jit(solution)/shard_map/ppermute | solution.py:18
  14.8 56.7 %collective-permute-start.2 = (bf16[512,1344]{0,1:T(8,128)(2,1)}, bf16[512,1344]{0,1:T(8,128)(2,1)}, u32[]{:S(2)}, u32[]{:S(2)}) collective-permute-start(bf16[512,1344]{0,1:T(8,128)(2,1)} %param.9), channel_id=1, source_target_pairs={{0,3},{1,0},{2,1},{3,2},{4,7},{5,4},{6,5},{7,6},{8,11},{9,8},{10,9... | collective-permute-start | bytes 4128776 | tf_op jit(solution)/shard_map/ppermute | solution.py:20
  46.8 18.1 %collective-permute-start.1 = (bf16[512,1344]{0,1:T(8,128)(2,1)}, bf16[512,1344]{0,1:T(8,128)(2,1)}, u32[]{:S(2)}, u32[]{:S(2)}) collective-permute-start(bf16[512,1344]{0,1:T(8,128)(2,1)} %collective-permute-done), channel_id=1, source_target_pairs={{0,1},{1,2},{2,3},{3,0},{4,5},{5,6},{6,7},{7,4},{8,9},{9,10},{10,1... | collective-permute-start | bytes 4128776 | tf_op jit(solution)/shard_map/ppermute | solution.py:18
  47.8 22.6 %copy-start.2 = (bf16[512,1344]{0,1:T(8,128)(2,1)S(1)}, bf16[512,1344]{0,1:T(8,128)(2,1)}, u32[]{:S(2)}) copy-start(bf16[512,1344]{0,1:T(8,128)(2,1)} %param.9) | copy-start | bytes 4128772
  47.8 439.9 %all-gather.15.cloned.1.call-start = ((), (), s32[]{:S(2)}) async-start(), calls=%async_computation.1 | async-start | bytes 2621440 | tf_op jit(solution)/shard_map/all_gather | solution.py:241
  69.9 175.9 %collective-permute-start.7 = (bf16[4,1344,256]{2,1,0:T(8,128)(2,1)}, bf16[4,1344,256]{2,1,0:T(8,128)(2,1)}, u32[]{:S(2)}, u32[]{:S(2)}) collective-permute-start(bf16[4,1344,256]{2,1,0:T(8,128)(2,1)} %bitcast.151), channel_id=1, source_target_pairs={{0,16},{16,0},{1,17},{17,1},{2,18},{18,2},{3,19},{19,3},{4,20},{20... | collective-permute-start | bytes 8257544 | tf_op jit(solution)/shard_map/ppermute | solution.py:137
  122.9 133.9 %collective-permute-start.10 = (bf16[4,1344,256]{2,1,0:T(8,128)(2,1)}, bf16[4,1344,256]{2,1,0:T(8,128)(2,1)}, u32[]{:S(2)}, u32[]{:S(2)}) collective-permute-start(bf16[4,1344,256]{2,1,0:T(8,128)(2,1)} %bitcast.139), channel_id=1, source_target_pairs={{0,16},{16,0},{1,17},{17,1},{2,18},{18,2},{3,19},{19,3},{4,20},{20... | collective-permute-start | bytes 8257544 | tf_op jit(solution)/shard_map/ppermute | solution.py:137
  225.1 120.6 %collective-permute-start.13 = (bf16[4,1344,512]{2,1,0:T(8,128)(2,1)}, bf16[4,1344,512]{2,1,0:T(8,128)(2,1)}, u32[]{:S(2)}, u32[]{:S(2)}) collective-permute-start(bf16[4,1344,512]{2,1,0:T(8,128)(2,1)} %bitcast.134), channel_id=1, source_target_pairs={{0,16},{16,0},{1,17},{17,1},{2,18},{18,2},{3,19},{19,3},{4,20},{20... | collective-permute-start | bytes 16515080 | tf_op jit(solution)/shard_map/ppermute | solution.py:137
  229.4 7.7 %copy-start.3 = (bf16[5376,256]{1,0:T(8,128)(2,1)S(1)}, bf16[5376,256]{1,0:T(8,128)(2,1)}, u32[]{:S(2)}) copy-start(bf16[5376,256]{1,0:T(8,128)(2,1)} %all-gather.19.cloned.1.call-done) | copy-start | bytes 8257540
  240.0 5.8 %copy-start.12 = (f32[5376]{0:T(1024)S(1)}, f32[5376]{0:T(1024)}, u32[]{:S(2)}) copy-start(f32[5376]{0:T(1024)} %param.10) | copy-start | bytes 64516
  252.9 17.9 %collective-permute-start.8 = (bf16[512,256]{1,0:T(8,128)(2,1)}, bf16[512,256]{1,0:T(8,128)(2,1)}, u32[]{:S(2)}, u32[]{:S(2)}) collective-permute-start(bf16[512,256]{1,0:T(8,128)(2,1)} %convolution_convert_fusion), channel_id=1, source_target_pairs={{0,8},{4,12},{1,9},{5,13},{2,10},{6,14},{3,11},{7,15},{16,24},{20,... | collective-permute-start | bytes 786440 | tf_op jit(solution)/shard_map/ppermute | solution.py:28
  254.2 48.7 %collective-permute-start.9 = (bf16[512,256]{1,0:T(8,128)(2,1)}, bf16[512,256]{1,0:T(8,128)(2,1)}, u32[]{:S(2)}, u32[]{:S(2)}) collective-permute-start(bf16[512,256]{1,0:T(8,128)(2,1)} %convolution_convert_fusion), channel_id=1, source_target_pairs={{0,4},{4,8},{8,12},{1,5},{5,9},{9,13},{2,6},{6,10},{10,14},{3,7},{... | collective-permute-start | bytes 786440 | tf_op jit(solution)/shard_map/ppermute | solution.py:28
  260.1 5.0 copy-start.9
  266.8 96.1 %collective-permute-start.11 = (bf16[512,256]{0,1:T(8,128)(2,1)}, bf16[512,256]{0,1:T(8,128)(2,1)}, u32[]{:S(2)}, u32[]{:S(2)}) collective-permute-start(bf16[512,256]{0,1:T(8,128)(2,1)} %bitcast.28), channel_id=1, source_target_pairs={{0,8},{4,12},{1,9},{5,13},{2,10},{6,14},{3,11},{7,15},{16,24},{20,... | collective-permute-start | bytes 786440 | tf_op jit(solution)/shard_map/ppermute | solution.py:28
  268.1 94.9 %collective-permute-start.12 = (bf16[512,256]{0,1:T(8,128)(2,1)}, bf16[512,256]{0,1:T(8,128)(2,1)}, u32[]{:S(2)}, u32[]{:S(2)}) collective-permute-start(bf16[512,256]{0,1:T(8,128)(2,1)} %bitcast.28), channel_id=1, source_target_pairs={{0,4},{4,8},{8,12},{1,5},{5,9},{9,13},{2,6},{6,10},{10,14},{3,7},{... | collective-permute-start | bytes 786440 | tf_op jit(solution)/shard_map/ppermute | solution.py:28
  305.2 8.4 %copy-start.13 = (f32[5376]{0:T(1024)S(1)}, f32[5376]{0:T(1024)}, u32[]{:S(2)}) copy-start(f32[5376]{0:T(1024)} %param.10) | copy-start | bytes 64516
  354.0 7.6 %copy-start.4 = (f32[512,4,128]{0,2,1:T(8,128)S(1)}, f32[512,4,128]{0,2,1:T(8,128)}, u32[]{:S(2)}) copy-start(f32[512,4,128]{0,2,1:T(8,128)} %get-tuple-element.28) | copy-start | bytes 3145732
  354.0 7.6 %copy-start.10 = (f32[128]{0:T(128)S(1)}, f32[128]{0:T(128)}, u32[]{:S(2)}) copy-start(f32[128]{0:T(128)} %param.14) | copy-start | bytes 1540
  363.0 11.0 %copy-start.6 = (bf16[1536,256]{0,1:T(8,128)(2,1)S(1)}, bf16[1536,256]{0,1:T(8,128)(2,1)}, u32[]{:S(2)}) copy-start(bf16[1536,256]{0,1:T(8,128)(2,1)} %copy.68) | copy-start | bytes 2359300
  374.0 6.7 %copy-start.14 = (f32[5376]{0:T(1024)S(1)}, f32[5376]{0:T(1024)}, u32[]{:S(2)}) copy-start(f32[5376]{0:T(1024)} %param.10) | copy-start | bytes 64516
  380.4 10.8 %copy-start.7 = (bf16[512,2,64]{0,2,1:T(8,128)(2,1)S(1)}, bf16[512,2,64]{0,2,1:T(8,128)(2,1)}, u32[]{:S(2)}) copy-start(bf16[512,2,64]{0,2,1:T(8,128)(2,1)} %get-tuple-element.10) | copy-start | bytes 393220
  380.4 69.3 %copy-start.5 = (pred[512,1536]{0,1:T(8,128)(4,1)S(1)}, pred[512,1536]{0,1:T(8,128)(4,1)}, u32[]{:S(2)}) copy-start(pred[512,1536]{0,1:T(8,128)(4,1)} %fusion.25) | copy-start | bytes 2359300
  380.4 112.7 %all-gather.13.cloned.1.call-start = ((), (), s32[]{:S(2)}) async-start(), calls=%async_computation | async-start | bytes 2621440 | tf_op jit(solution)/shard_map/all_gather | solution.py:241
  387.1 17.6 %collective-permute-start.3 = (bf16[512,256]{1,0:T(8,128)(2,1)S(1)}, bf16[512,256]{1,0:T(8,128)(2,1)S(1)}, u32[]{:S(2)}, u32[]{:S(2)}) collective-permute-start(bf16[512,256]{1,0:T(8,128)(2,1)S(1)} %convolution_convert_fusion.1), channel_id=1, source_target_pairs={{0,8},{4,12},{1,9},{5,13},{2,10},{6,14},{3,11},{7,15},{16,24},{20,... | collective-permute-start | bytes 786440 | tf_op jit(solution)/shard_map/ppermute | solution.py:28
  388.4 46.7 %collective-permute-start.4 = (bf16[512,256]{1,0:T(8,128)(2,1)S(1)}, bf16[512,256]{1,0:T(8,128)(2,1)S(1)}, u32[]{:S(2)}, u32[]{:S(2)}) collective-permute-start(bf16[512,256]{1,0:T(8,128)(2,1)S(1)} %convolution_convert_fusion.1), channel_id=1, source_target_pairs={{0,4},{4,8},{8,12},{1,5},{5,9},{9,13},{2,6},{6,10},{10,14},{3,7},{... | collective-permute-start | bytes 786440 | tf_op jit(solution)/shard_map/ppermute | solution.py:28
  392.0 44.0 %collective-permute-start.5 = (bf16[512,256]{0,1:T(8,128)(2,1)}, bf16[512,256]{0,1:T(8,128)(2,1)}, u32[]{:S(2)}, u32[]{:S(2)}) collective-permute-start(bf16[512,256]{0,1:T(8,128)(2,1)} %bitcast.6), channel_id=1, source_target_pairs={{0,8},{4,12},{1,9},{5,13},{2,10},{6,14},{3,11},{7,15},{16,24},{20,... | collective-permute-start | bytes 786440 | tf_op jit(solution)/shard_map/ppermute | solution.py:28
  393.2 56.5 %collective-permute-start.6 = (bf16[512,256]{0,1:T(8,128)(2,1)}, bf16[512,256]{0,1:T(8,128)(2,1)}, u32[]{:S(2)}, u32[]{:S(2)}) collective-permute-start(bf16[512,256]{0,1:T(8,128)(2,1)} %bitcast.6), channel_id=1, source_target_pairs={{0,4},{4,8},{8,12},{1,5},{5,9},{9,13},{2,6},{6,10},{10,14},{3,7},{... | collective-permute-start | bytes 786440 | tf_op jit(solution)/shard_map/ppermute | solution.py:28
  482.6 61.8 %collective-permute-start.14 = (bf16[4,256,1344]{1,2,0:T(8,128)(2,1)S(1)}, bf16[4,256,1344]{1,2,0:T(8,128)(2,1)}, u32[]{:S(2)}, u32[]{:S(2)}) collective-permute-start(bf16[4,256,1344]{1,2,0:T(8,128)(2,1)S(1)} %copy.75), channel_id=1, source_target_pairs={{0,16},{16,0},{1,17},{17,1},{2,18},{18,2},{3,19},{19,3},{4,20},{20... | collective-permute-start | bytes 8257544 | tf_op jit(solution)/shard_map/ppermute | solution.py:137
  493.1 51.3 %copy-start.11 = (bf16[512,2048]{0,1:T(8,128)(2,1)S(1)}, bf16[512,2048]{0,1:T(8,128)(2,1)}, u32[]{:S(2)}) copy-start(bf16[512,2048]{0,1:T(8,128)(2,1)} %all-gather.15.cloned.1.call-done) | copy-start | bytes 6291460
  500.4 55.1 %copy-start.8 = (f32[1344]{0:T(1024)S(1)}, f32[1344]{0:T(1024)}, u32[]{:S(2)}) copy-start(f32[1344]{0:T(1024)} %param.17) | copy-start | bytes 16132
  544.4 14.8 %copy-start.1 = (bf16[1024,1344]{0,1:T(8,128)(2,1)S(1)}, bf16[1024,1344]{0,1:T(8,128)(2,1)}, u32[]{:S(2)}) copy-start(bf16[1024,1344]{0,1:T(8,128)(2,1)} %param.16) | copy-start | bytes 8257540
Sparse Core Ops, SparseCore 0:
  8.9 56.6 all-gather.16
  67.2 55.6 all-gather.18
  124.4 100.6 all-gather.20
  226.5 118.9 all-gather.22
  347.0 89.8 all-gather.24
  438.3 27.7 all-gather.14
  467.6 22.4 all-gather.12
